TPU v7x, 256 devices: a whole 4x4x8 slice. The times are simulated.
256 devices in a mesh: row: 32 (over z_lo, y, core), col: 8 (over z_hi, x).
Axes of the slice: x: 4, y: 4, z: 8 (z_hi: 2, z_lo: 4; z = z_hi * 4 + z_lo), core: 2. Of those that a mesh axis runs over, the one named last changes fastest.
Arguments:
- weights: bfloat16 [8192, 32768], P('row', 'col'), may hold values from -6 to 6
- panel_first: float32 [256, 32768], P('row', 'col'), may hold values from -1 to 2, as said below
- panel_second: float32 [256, 32768], P('row', 'col'), may hold values from -1 to 2, as said below
- removed_first: int32 [512], P('col'), may hold values from -1 to 4095, as said below
- removed_second: int32 [512], P('col'), may hold values from -1 to 4095, as said below
Outputs:
- pruned: bfloat16 [8192, 32768], P('row', 'col')
Inputs may be any that keep to these rules, and one draw needn't show every extreme that they name: `removed_first`: in each list every owner's live slots come first; there are 256 live slots in all, at most 64 for one owner and exactly 64 for some owner; live values of one owner are distinct, and the two lists name no column twice. `removed_second`: same form as removed_first, with its own owners. `panel_first`: together with panel_second, its entries at the columns S1 and S2 are the rows of one symmetric positive definite matrix of order 2 * 256. `panel_second`: rows of the same inverse Hessian as panel_first, for the columns S2.
All inputs are finite; a program needn't handle non-finite values.
Results may differ from a plain program's by a relative error of at most 0.001.
Values may be sent and summed in bfloat16 or wider, within the bound.
No kernel may reach another device: no remote copies, remote signals or barrier semaphores. Data moves between devices by JAX's collectives and lax.ppermute only.
A program may use at most 64 MiB of HBM per device.

v0:
```python
import jax
import jax.numpy as jnp
from jax import lax
from jax.sharding import PartitionSpec as P

highest = lax.Precision.HIGHEST


def pick_columns(matrix, chosen):
    present = chosen >= 0
    column = jnp.where(present, chosen, 0)
    taken = jnp.take(matrix, column, axis=1)
    return jnp.where(present[None, :], taken, jnp.zeros((), matrix.dtype))


def compactor(gathered, total):
    present = gathered >= 0
    position = jnp.cumsum(present.astype(jnp.int32)) - 1
    target = jnp.arange(total, dtype=jnp.int32)
    return (present[:, None] & (position[:, None] == target[None, :])).astype(jnp.float32)


def apply_inverse(factor, matrix):
    return jax.scipy.linalg.cho_solve((factor, True), matrix.T).T


def on_device(weights, panel_first, panel_second, removed_first, removed_second):
    panel_rows = panel_first.shape[0]
    slot_count = removed_first.shape[0]
    row_devices = lax.axis_size("row")
    col_devices = lax.axis_size("col")
    order = panel_rows * row_devices
    lists_first, lists_second = (
        lax.all_gather(removed_first, "col", axis=0, tiled=True),
        lax.all_gather(removed_second, "col", axis=0, tiled=True),
    )
    pack_first = compactor(lists_first, order)
    pack_second = compactor(lists_second, order)
    stacked = jnp.stack([panel_first, panel_second])
    chosen = jnp.concatenate([removed_first, removed_second])
    present = chosen >= 0
    column = jnp.where(present, chosen, 0)
    local_entries = jnp.where(present[None, None, :], jnp.take(stacked, column, axis=2), 0.0)
    everyone = lax.all_gather(local_entries[None], ("row", "col"), axis=0, tiled=True)
    everyone = everyone.reshape(row_devices, col_devices, 2, panel_rows, 2, slot_count)
    everyone = jnp.transpose(everyone, (2, 4, 0, 3, 1, 5)).reshape(
        2, 2, order, col_devices * slot_count
    )
    h_first = jnp.dot(everyone[0, 0], pack_first, precision=highest)
    first_at_second = jnp.dot(everyone[0, 1], pack_second, precision=highest)
    second_at_first = jnp.dot(everyone[1, 0], pack_first, precision=highest)
    second_at_second = jnp.dot(everyone[1, 1], pack_second, precision=highest)
    factor_first = jnp.linalg.cholesky(h_first)
    coupling = apply_inverse(factor_first, second_at_first)
    h_second = second_at_second - jnp.dot(coupling, first_at_second, precision=highest)
    factor_second = jnp.linalg.cholesky(h_second)
    first_local = pick_columns(weights, removed_first)
    first_cols = lax.all_gather(first_local, "col", axis=1, tiled=True)
    w_first = jnp.dot(
        first_cols, pack_first.astype(jnp.bfloat16), preferred_element_type=jnp.float32
    )
    coef_first = apply_inverse(factor_first, w_first)
    panel_whole = lax.all_gather(panel_first, "row", axis=0, tiled=True)
    updated = weights.astype(jnp.float32) - jnp.dot(coef_first, panel_whole, precision=highest)
    panel_next = lax.all_gather(panel_second, "row", axis=0, tiled=True) - jnp.dot(
        coupling, panel_whole, precision=highest
    )
    second_local = pick_columns(updated, removed_second)
    second_cols = lax.all_gather(second_local, "col", axis=1, tiled=True)
    w_second = jnp.dot(second_cols, pack_second, precision=highest)
    coef_second = apply_inverse(factor_second, w_second)
    pruned = updated - jnp.dot(coef_second, panel_next, precision=highest)
    return pruned.astype(jnp.bfloat16)


def solution(mesh):
    return jax.shard_map(
        on_device,
        mesh=mesh,
        in_specs=(P("row", "col"), P("row", "col"), P("row", "col"), P("col"), P("col")),
        out_specs=P("row", "col"),
        check_vma=False,
    )
```

profile of v0, /device:TPU:96, one launch (start us, length us, event | category | flops | bytes accessed | tf_op | source)
XLA Modules:
  0.0 969.7 jit_solution(7421695014664704210)
XLA Ops:
  7.7 4.4 copy.21
  12.2 2.9 gather_fusion
  19.5 15.0 %all-reduce.3 = (s32[512]{0:T(512)S(1)}, s32[512]{0:T(512)S(1)}) all-reduce(s32[512]{0:T(512)S(1)} %dynamic-update-slice.10, s32[512]{0:T(512)S(1)} %dynamic-update-slice.11), channel_id=1, replica_groups=mesh['row'=32,'col'=8] {'col'}, use_global_device_ids=true, to_apply=%add.1 | all-reduce | flops 1024 | bytes 8192
  40.8 44.2 %all_gather.23 = bf16[256,512]{0,1:T(8,128)(2,1)S(1)} all-gather(bf16[256,64]{0,1:T(8,128)(2,1)S(1)} %select_bitcast_fusion.3), channel_id=1, replica_groups=mesh['row'=32,'col'=8] {'col'}, dimensions={1}, use_global_device_ids=true | all-gather | bytes 294912 | tf_op jit(solution)/shard_map/all_gather | solution.py:58
  86.1 652.6 %all-gather.4.cloned.1.call-done = f32[256,2,8,128]{3,2,1,0:T(8,128)} async-done(((f32[1,2,8,128]{3,2,1,0:T(8,128)}), f32[256,2,8,128]{3,2,1,0:T(8,128)}) %all-gather.4.cloned.1.call-update) | async-done | bytes 2097168 | tf_op jit(solution)/shard_map/all_gather | solution.py:44
  738.7 5.6 reshape.193
  744.3 6.6 copy.33
  750.8 3.6 reshape.194
  755.8 11.7 %cholesky.130 = f32[128,128]{1,0:T(8,128)S(1)} custom-call(f32[128,128]{1,0:T(8,128)S(1)} %cholesky.194), custom_call_target="Cholesky" | custom-call | tf_op jit(solution)/shard_map/jit(cholesky)/cholesky | solution.py:53
  767.6 9.8 %custom-call.16 = f32[1,128,128]{1,2,0:T(8,128)S(1)} custom-call(f32[1,128,128]{2,1,0:T(8,128)S(1)} %get-tuple-element.67), custom_call_target="InvertDiagBlocksLowerTriangular" | custom-call | tf_op jit(solution)/shard_map/jit(cholesky)/cholesky | solution.py:53
  777.9 11.7 %cholesky.147 = f32[128,128]{1,0:T(8,128)S(1)} custom-call(f32[128,128]{1,0:T(8,128)S(1)} %convolution_subtract_fusion.11), custom_call_target="Cholesky" | custom-call | tf_op jit(solution)/shard_map/jit(cholesky)/cholesky | solution.py:53
  791.6 3.7 while.6
  795.3 19.9 %custom-call.17 = f32[2,128,128]{1,2,0:T(8,128)S(1)} custom-call(f32[2,128,128]{2,1,0:T(8,128)S(1)} %get-tuple-element.27), custom_call_target="InvertDiagBlocksLowerTriangular" | custom-call | tf_op jit(solution)/shard_map/jit(_cho_solve)/triangular_solve | solution.py:24
  819.8 11.7 %cholesky.164 = f32[128,128]{1,0:T(8,128)S(1)} custom-call(f32[128,128]{1,0:T(8,128)S(1)} %cholesky.197), custom_call_target="Cholesky" | custom-call | tf_op jit(solution)/shard_map/jit(cholesky)/cholesky | solution.py:56
  831.6 9.8 %custom-call.19 = f32[1,128,128]{1,2,0:T(8,128)S(1)} custom-call(f32[1,128,128]{2,1,0:T(8,128)S(1)} %get-tuple-element.63), custom_call_target="InvertDiagBlocksLowerTriangular" | custom-call | tf_op jit(solution)/shard_map/jit(cholesky)/cholesky | solution.py:56
  843.6 12.1 %cholesky.181 = f32[128,128]{1,0:T(8,128)S(1)} custom-call(f32[128,128]{1,0:T(8,128)S(1)} %convolution_subtract_fusion.10), custom_call_target="Cholesky" | custom-call | tf_op jit(solution)/shard_map/jit(cholesky)/cholesky | solution.py:56
  858.2 3.7 while.7
  862.0 19.7 %custom-call.20 = f32[2,128,128]{1,2,0:T(8,128)S(1)} custom-call(f32[2,128,128]{2,1,0:T(8,128)S(1)} %get-tuple-element.29), custom_call_target="InvertDiagBlocksLowerTriangular" | custom-call | tf_op jit(solution)/shard_map/jit(_cho_solve)/triangular_solve | solution.py:24
  885.3 8.3 convolution_subtract_fusion.2
  893.5 5.6 copy.29
  899.2 2.8 gather_fusion.2
  902.1 45.2 %all_gather.26 = f32[256,512]{0,1:T(8,128)S(1)} all-gather(f32[256,64]{0,1:T(8,128)S(1)} %select_bitcast_fusion.2), channel_id=1, replica_groups=mesh['row'=32,'col'=8] {'col'}, dimensions={1}, use_global_device_ids=true | all-gather | bytes 589824 | tf_op jit(solution)/shard_map/all_gather | solution.py:69
  949.9 8.0 convolution_subtract_fusion.1
  957.9 5.1 fusion
  (115 shorter events, 36.5 us)
Async XLA Ops:
  6.5 11.2 %copy-start.6 = (u32[256]{0:T(256)S(1)}, u32[256]{0:T(256)}, u32[]{:S(2)}) copy-start(u32[256]{0:T(256)} %constant.149) | copy-start | bytes 3076
  6.5 5.5 copy-start.4
  6.5 5.5 copy-start.5
  6.5 29.1 %copy-start.1 = (bf16[256,4096]{1,0:T(8,128)(2,1)S(1)}, bf16[256,4096]{1,0:T(8,128)(2,1)}, u32[]{:S(2)}) copy-start(bf16[256,4096]{1,0:T(8,128)(2,1)} %param.8) | copy-start | bytes 6291460
  6.5 732.1 %all-gather.4.cloned.1.call-start = ((), (), s32[]{:S(2)}) async-start(), calls=%async_computation | async-start | bytes 2105344 | tf_op jit(solution)/shard_map/all_gather | solution.py:44
  16.2 869.0 %all-gather.6.cloned.1.call-start = ((), (), s32[]{:S(2)}) async-start(), calls=%async_computation.1 | async-start | bytes 4325376 | tf_op jit(solution)/shard_map/all_gather | solution.py:63
  17.0 932.9 %all-gather.8.cloned.1.call-start = ((), (), s32[]{:S(2)}) async-start(), calls=%async_computation.2 | async-start | bytes 4325376 | tf_op jit(solution)/shard_map/all_gather | solution.py:65
  818.3 67.0 %copy-start.2 = (bf16[256,4096]{1,0:T(8,128)(2,1)S(1)}, bf16[256,4096]{1,0:T(8,128)(2,1)}, u32[]{:S(2)}) copy-start(bf16[256,4096]{1,0:T(8,128)(2,1)} %param.8) | copy-start | bytes 6291460
  819.1 0.7 copy-start.3
  949.9 8.0 copy-start
Sparse Core Ops, SparseCore 0:
  16.4 722.2 all-gather.3
  740.5 55.9 all-gather.5
  798.3 62.1 all-gather.7
where the time goes:
time: 977 us; the launch traced here: 970 us
  waiting for transfers between devices  654 us (67%)
  other arithmetic  111 us (11%)
  blocking collectives  104 us (11%)
  local copies, waits for them, and re-layouts  47.1 us (5%)
  matrix products  35.8 us (4%)
  between operations  16.9 us (2%)
    all_gather x1, waiting for transfers between devices, on_device(): lax.all_gather(local_entries[None], ('row', 'col'), axis=0, tiled=True)  653 us
    all_gather x1, blocking collectives, on_device(): second_cols = lax.all_gather(second_local, 'col', axis=1, tiled=True)  45.2 us
    all_gather x1, blocking collectives, on_device(): first_cols = lax.all_gather(first_local, 'col', axis=1, tiled=True)  44.2 us
    another operation x5, other arithmetic, apply_inverse(): return jax.scipy.linalg.cho_solve((factor, True), matrix.T).T  39.6 us
    another operation x7, other arithmetic, on_device(): factor_second = jnp.linalg.cholesky(h_second)  34.9 us
    another operation x6, other arithmetic, on_device(): factor_first = jnp.linalg.cholesky(h_first)  34 us
  transfers between devices with their start and end apart: 3, of which 1 were waited for; matrix products, arithmetic and copies ran while one was open for 18% of the time, Pallas kernels for 0%

commit v1 on v0

--- a/solution.py
+++ b/solution.py
@@ -41,7 +41,12 @@
     present = chosen >= 0
     column = jnp.where(present, chosen, 0)
     local_entries = jnp.where(present[None, None, :], jnp.take(stacked, column, axis=2), 0.0)
-    everyone = lax.all_gather(local_entries[None], ("row", "col"), axis=0, tiled=True)
+    everyone = jnp.concatenate(
+        lax.all_to_all(
+            jnp.stack([local_entries[None]] * lax.axis_size(("row", "col"))), ("row", "col"), 0, 0
+        ),
+        axis=0,
+    )
     everyone = everyone.reshape(row_devices, col_devices, 2, panel_rows, 2, slot_count)
     everyone = jnp.transpose(everyone, (2, 4, 0, 3, 1, 5)).reshape(
         2, 2, order, col_devices * slot_count

time: 977 us -> 390 us (0.40)
  the two profiles are of different devices: /device:TPU:96 before, /device:TPU:6 now
where the time goes in v1:
time: 390 us; the launch traced here: 382 us
  blocking collectives  154 us (39%)
  other arithmetic  111 us (28%)
  local copies, waits for them, and re-layouts  47.7 us (12%)
  matrix products  35.8 us (9%)
  between operations  17.2 us (4%)
  starting transfers between devices  14.7 us (4%)
    unnamed x1, blocking collectives  64.7 us
    all_gather x1, blocking collectives, on_device(): second_cols = lax.all_gather(second_local, 'col', axis=1, tiled=True)  45.1 us
    all_gather x1, blocking collectives, on_device(): first_cols = lax.all_gather(first_local, 'col', axis=1, tiled=True)  44.6 us
    another operation x5, other arithmetic, apply_inverse(): return jax.scipy.linalg.cho_solve((factor, True), matrix.T).T  39.6 us
    another operation x7, other arithmetic, on_device(): factor_second = jnp.linalg.cholesky(h_second)  34.9 us
    another operation x6, other arithmetic, on_device(): factor_first = jnp.linalg.cholesky(h_first)  34 us
    all_to_all x1, starting transfers between devices, on_device(): lax.all_to_all(jnp.stack([local_entries[None]] * lax.axis_size(('row', 'c...  14.6 us
    dot_general x1, matrix products, on_device(): jnp.dot(coef_first, panel_whole, precision=highest)  8.27 us
  transfers between devices with their start and end apart: 3, of which 0 were waited for; matrix products, arithmetic and copies ran while one was open for 47% of the time, Pallas kernels for 0%

profile of v1, /device:TPU:6, one launch (start us, length us, event | category | flops | bytes accessed | tf_op | source)
XLA Modules:
  0.0 382.5 jit_solution(6752058354706420848)
XLA Ops:
  8.2 4.4 %copy.31 = f32[2,8,4096]{1,0,2:T(2,128)} copy(f32[2,8,4096]{2,1,0:T(8,128)S(1)} %pad_maximum_fusion) | data formatting | bytes 524288 | tf_op jit(solution)/shard_map/stack | solution.py:39
  12.7 2.9 gather_fusion
  17.7 14.6 %all-to-all-start = ((f32[256,1,2,8,128]{4,3,2,1,0:T(8,128)}), f32[256,1,2,8,128]{4,3,2,1,0:T(8,128)S(1)}, u32[]{:S(2)}, u32[]{:S(2)}) async-start(f32[256,1,2,8,128]{4,3,2,1,0:T(8,128)} %stack.15), calls=%async_computation | async-start | bytes 4194304 | tf_op jit(solution)/shard_map/all_to_all | solution.py:45
  34.8 64.7 %all-reduce.3 = (s32[512]{0:T(512)S(1)}, s32[512]{0:T(512)S(1)}) all-reduce(s32[512]{0:T(512)S(1)} %dynamic-update-slice.10, s32[512]{0:T(512)S(1)} %dynamic-update-slice.11), channel_id=1, replica_groups=mesh['row'=32,'col'=8] {'col'}, use_global_device_ids=true, to_apply=%add.1 | all-reduce | flops 1024 | bytes 8192
  100.3 4.1 %copy.35 = bf16[256,4096]{0,1:T(8,128)(2,1)} copy(bf16[256,4096]{1,0:T(8,128)(2,1)} %param.8) | data formatting | bytes 4194304 | tf_op args[0]
  107.3 44.6 %all_gather.19 = bf16[256,512]{0,1:T(8,128)(2,1)S(1)} all-gather(bf16[256,64]{0,1:T(8,128)(2,1)S(1)} %select_bitcast_fusion.4), channel_id=1, replica_groups=mesh['row'=32,'col'=8] {'col'}, dimensions={1}, use_global_device_ids=true | all-gather | bytes 294912 | tf_op jit(solution)/shard_map/all_gather | solution.py:63
  153.2 3.6 reshape_reshape.3
  156.8 6.6 %copy.33 = f32[2,2,32,8,8,64]{5,4,3,2,1,0:T(8,128)} copy(f32[2,2,32,8,8,64]{5,1,3,0,4,2:T(2,128)} %bitcast.130) | data formatting | bytes 4194304 | tf_op jit(solution)/shard_map/transpose | solution.py:51
  163.4 3.6 reshape.187
  168.4 11.7 %cholesky.130 = f32[128,128]{1,0:T(8,128)S(1)} custom-call(f32[128,128]{1,0:T(8,128)S(1)} %cholesky.194), custom_call_target="Cholesky" | custom-call | tf_op jit(solution)/shard_map/jit(cholesky)/cholesky | solution.py:58
  180.1 9.8 %custom-call.16 = f32[1,128,128]{1,2,0:T(8,128)S(1)} custom-call(f32[1,128,128]{2,1,0:T(8,128)S(1)} %get-tuple-element.67), custom_call_target="InvertDiagBlocksLowerTriangular" | custom-call | tf_op jit(solution)/shard_map/jit(cholesky)/cholesky | solution.py:58
  190.4 11.7 %cholesky.147 = f32[128,128]{1,0:T(8,128)S(1)} custom-call(f32[128,128]{1,0:T(8,128)S(1)} %convolution_subtract_fusion.11), custom_call_target="Cholesky" | custom-call | tf_op jit(solution)/shard_map/jit(cholesky)/cholesky | solution.py:58
  204.2 3.7 while.6
  207.9 19.9 %custom-call.17 = f32[2,128,128]{1,2,0:T(8,128)S(1)} custom-call(f32[2,128,128]{2,1,0:T(8,128)S(1)} %get-tuple-element.27), custom_call_target="InvertDiagBlocksLowerTriangular" | custom-call | tf_op jit(solution)/shard_map/jit(_cho_solve)/triangular_solve | solution.py:24
  232.4 11.7 %cholesky.164 = f32[128,128]{1,0:T(8,128)S(1)} custom-call(f32[128,128]{1,0:T(8,128)S(1)} %cholesky.197), custom_call_target="Cholesky" | custom-call | tf_op jit(solution)/shard_map/jit(cholesky)/cholesky | solution.py:61
  244.2 9.8 %custom-call.19 = f32[1,128,128]{1,2,0:T(8,128)S(1)} custom-call(f32[1,128,128]{2,1,0:T(8,128)S(1)} %get-tuple-element.63), custom_call_target="InvertDiagBlocksLowerTriangular" | custom-call | tf_op jit(solution)/shard_map/jit(cholesky)/cholesky | solution.py:61
  256.1 12.1 %cholesky.181 = f32[128,128]{1,0:T(8,128)S(1)} custom-call(f32[128,128]{1,0:T(8,128)S(1)} %convolution_subtract_fusion.10), custom_call_target="Cholesky" | custom-call | tf_op jit(solution)/shard_map/jit(cholesky)/cholesky | solution.py:61
  270.8 3.7 while.7
  274.5 19.7 %custom-call.20 = f32[2,128,128]{1,2,0:T(8,128)S(1)} custom-call(f32[2,128,128]{2,1,0:T(8,128)S(1)} %get-tuple-element.29), custom_call_target="InvertDiagBlocksLowerTriangular" | custom-call | tf_op jit(solution)/shard_map/jit(_cho_solve)/triangular_solve | solution.py:24
  297.8 8.3 %convolution_subtract_fusion.2 = f32[256,4096]{1,0:T(8,128)} fusion(f32[256,4096]{1,0:T(8,128)} %all-gather.3.cloned.1.call-done, bf16[256,4096]{1,0:T(8,128)(2,1)S(1)} %copy-done.1, f32[128,256]{1,0:T(8,128)S(1)} %fusion.56, f32[128,256]{1,0:T(8,128)S(1)} %fusion.53), kind=kOutput, calls=%fused_computation.9 | convolution fusion | flops 3223388160 | bytes 10747904 | tf_op jit(solution)/shard_map/dot_general | solution.py:69
  306.1 5.6 %copy.39 = f32[256,4096]{0,1:T(8,128)} copy(f32[256,4096]{1,0:T(8,128)} %convolution_subtract_fusion.2) | data formatting | bytes 8388608 | tf_op jit(solution)/shard_map/sub | solution.py:69
  314.7 45.1 %all_gather.22 = f32[256,512]{0,1:T(8,128)S(1)} all-gather(f32[256,64]{0,1:T(8,128)S(1)} %select_bitcast_fusion.3), channel_id=1, replica_groups=mesh['row'=32,'col'=8] {'col'}, dimensions={1}, use_global_device_ids=true | all-gather | bytes 589824 | tf_op jit(solution)/shard_map/all_gather | solution.py:74
  362.4 8.0 %convolution_subtract_fusion.1 = f32[256,4096]{1,0:T(8,128)S(1)} fusion(f32[256,4096]{1,0:T(8,128)} %all-gather.5.cloned.1.call-done, f32[256,4096]{1,0:T(8,128)} %all-gather.3.cloned.1.call-done, f32[128,256]{1,0:T(8,128)S(1)} %fusion.54, f32[128,256]{1,0:T(8,128)S(1)} %fusion.52), kind=kOutput, calls=%fused_computation.8 | convolution fusion | flops 3222339584 | bytes 12845056 | tf_op jit(solution)/shard_map/dot_general | solution.py:70
  370.4 5.1 %fusion = bf16[256,4096]{1,0:T(8,128)(2,1)} fusion(f32[256,4096]{1,0:T(8,128)S(1)} %copy-done, f32[256,4096]{1,0:T(8,128)S(1)} %convolution_subtract_fusion.1, f32[128,256]{1,0:T(8,128)S(1)} %fusion.48, f32[128,256]{1,0:T(8,128)S(1)} %fusion.47), kind=kOutput, calls=%fused_computation.10 | convolution fusion | flops 3223388160 | bytes 10747904 | tf_op jit(solution)/shard_map/dot_general | solution.py:77
  (113 shorter events, 37.6 us)
Async XLA Ops:
  6.5 6.1 %copy-start.3 = (s32[64]{0:T(128)S(1)}, s32[64]{0:T(128)}, u32[]{:S(2)}) copy-start(s32[64]{0:T(128)} %param.11) | copy-start | bytes 772
  6.5 6.1 %copy-start.4 = (s32[64]{0:T(128)S(1)}, s32[64]{0:T(128)}, u32[]{:S(2)}) copy-start(s32[64]{0:T(128)} %param.12) | copy-start | bytes 772
  6.5 291.3 %all-gather.3.cloned.1.call-start = ((), (), s32[]{:S(2)}) async-start(), calls=%async_computation.1 | async-start | bytes 4325376 | tf_op jit(solution)/shard_map/all_gather | solution.py:68
  12.6 20.5 %copy-start.5 = (u32[256]{0:T(256)S(1)}, u32[256]{0:T(256)}, u32[]{:S(2)}) copy-start(u32[256]{0:T(256)} %constant.149) | copy-start | bytes 3076
  17.7 135.5 %all-to-all-start = ((f32[256,1,2,8,128]{4,3,2,1,0:T(8,128)}), f32[256,1,2,8,128]{4,3,2,1,0:T(8,128)S(1)}, u32[]{:S(2)}, u32[]{:S(2)}) async-start(f32[256,1,2,8,128]{4,3,2,1,0:T(8,128)} %stack.15), calls=%async_computation | async-start | bytes 4194304 | tf_op jit(solution)/shard_map/all_to_all | solution.py:45
  32.3 330.0 %all-gather.5.cloned.1.call-start = ((), (), s32[]{:S(2)}) async-start(), calls=%async_computation.2 | async-start | bytes 4325376 | tf_op jit(solution)/shard_map/all_gather | solution.py:70
  230.9 66.9 %copy-start.1 = (bf16[256,4096]{1,0:T(8,128)(2,1)S(1)}, bf16[256,4096]{1,0:T(8,128)(2,1)}, u32[]{:S(2)}) copy-start(bf16[256,4096]{1,0:T(8,128)(2,1)} %param.8) | copy-start | bytes 6291460
  231.7 0.7 copy-start.2
  362.4 8.0 %copy-start = (f32[256,4096]{1,0:T(8,128)S(1)}, f32[256,4096]{1,0:T(8,128)}, u32[]{:S(2)}) copy-start(f32[256,4096]{1,0:T(8,128)} %convolution_subtract_fusion.2) | copy-start | bytes 12582916
Sparse Core Ops, SparseCore 0:
  9.2 93.4 all-gather.2
  104.6 61.7 all-gather.4
